TPU v7x, 128 devices: a whole 4x4x4 slice. The times are simulated.
128 devices in a mesh: req: 8 (over y, core), tok: 16 (over x, z).
Axes of the slice: x: 4, y: 4, z: 4, core: 2. Of those that a mesh axis runs over, the one named last changes fastest.
Arguments:
- layer_input: bfloat16 [16384, 2048], P(('req', 'tok')), may hold values from -12 to 12
- q_in: bfloat16 [16384, 2048], P(('req', 'tok')), may hold values from -10 to 10
- k_in: bfloat16 [16384, 2048], P(('req', 'tok')), may hold values from -10 to 10
- v_in: bfloat16 [16384, 2048], P(('req', 'tok')), may hold values from -6 to 6
- segment_ids: int32 [8, 2048], P('req'), may hold values from 0 to 3, never falling along the last dimension, each value on 1 to 1024 neighbouring positions
- lambda_parts: float32 [4, 128], replicated, may hold values from -0.8 to 0.8
- out_weight: bfloat16 [2048, 2048], replicated, may hold values from -0.125 to 0.125
- ffn_gain: float32 [2048], replicated, may hold values from 0.1 to 1.9
- gate_weight: bfloat16 [2048, 5632], P(None, 'req'), may hold values from -0.125 to 0.125
- up_weight: bfloat16 [2048, 5632], P(None, 'req'), may hold values from -0.125 to 0.125
- down_weight: bfloat16 [5632, 2048], P('req'), may hold values from -0.078125 to 0.078125
- next_gain: float32 [2048], replicated, may hold values from 0.1 to 1.9
- qkv_weight: bfloat16 [2048, 6144], P(None, 'req'), may hold values from -0.125 to 0.125
- page_owner: int32 [8, 256], P('req'), may hold values from 0 to 15, as said below
- page_slot: int32 [8, 256], P('req'), may hold values from 0 to 15, as said below
Outputs:
- layer_output: bfloat16 [16384, 2048], P(('req', 'tok'))
- q_next: bfloat16 [16384, 2048], P(('req', 'tok'))
- page_cache: bfloat16 [2048, 8, 4096], P(('req', 'tok'))
Inputs may be any that keep to these rules, and one draw needn't show every extreme that they name: `segment_ids`: segment numbers never fall along a group; each of the 4 prompts of a group has 1 to 1024 tokens, one exactly 1024. `page_owner`: the 16 pages of each device name every device of its request group as owner exactly once. `page_slot`: within a request group every pair of owner and slot is named by exactly one page.
All inputs are finite; a program needn't handle non-finite values.
Results may differ from a plain program's by a relative error of at most 0.017.
Values may be sent and summed in bfloat16 or wider, within the bound.
A program may use at most 192 MiB of HBM per device.

v0:
```python
import math
import jax
import jax.numpy as jnp
from jax import lax
from jax.sharding import PartitionSpec as P

HEADS = 8
PAGE = 8
NEG_FILL = -1e30
LAMBDA_INIT = 0.2
EPSILON = 1e-05
MAX_SEG = 1024


def rms_rows(values):
    return values * lax.rsqrt(jnp.mean(values * values, axis=-1, keepdims=True) + EPSILON)


def lambda_value(lambda_parts):
    first_term = jnp.exp(jnp.sum(lambda_parts[0] * lambda_parts[1]))
    second_term = jnp.exp(jnp.sum(lambda_parts[2] * lambda_parts[3]))
    return first_term - second_term + LAMBDA_INIT


def body(
    layer_input,
    q_in,
    k_in,
    v_in,
    segment_ids,
    lambda_parts,
    out_weight,
    ffn_gain,
    gate_weight,
    up_weight,
    down_weight,
    next_gain,
    qkv_weight,
    page_owner,
    page_slot,
):
    row_count = q_in.shape[0]
    feat_width = q_in.shape[1]
    head_dim = feat_width // (2 * HEADS)
    peer_count = lax.axis_size("tok")
    tok_place = lax.axis_index("tok")
    seg_row = segment_ids[0]
    first_row = tok_place * row_count
    query_places = first_row + jnp.arange(row_count)
    query_segs = lax.dynamic_slice_in_dim(seg_row, first_row, row_count)
    lambda_mix = lambda_value(lambda_parts)
    score_scale = 1.0 / math.sqrt(head_dim)
    query_split = q_in.reshape(row_count, HEADS, 2, head_dim)
    run_max = jnp.full((HEADS, 2, row_count), NEG_FILL, jnp.float32)
    back = -(-(MAX_SEG - 1) // row_count)
    own_kv = jnp.concatenate([k_in, v_in], axis=1)
    all_kv = lax.all_gather(own_kv, "tok", axis=0, tiled=True)
    padded_kv = jnp.concatenate(
        [jnp.zeros((back * row_count, 2 * feat_width), all_kv.dtype), all_kv], axis=0
    )
    window = lax.dynamic_slice_in_dim(padded_kv, first_row, (back + 1) * row_count, 0)
    piece_len = window.shape[0]
    key_rows = window[:, :feat_width]
    value_rows = window[:, feat_width:]
    key_split = key_rows.reshape(piece_len, HEADS, 2, head_dim)
    value_split = value_rows.reshape(piece_len, HEADS, 2 * head_dim)
    key_places = (tok_place - back) * row_count + jnp.arange(piece_len)
    key_segs = jnp.take(seg_row, jnp.clip(key_places, 0, seg_row.shape[0] - 1))
    visible = (
        (key_places[None, :] >= 0)
        & (key_segs[None, :] == query_segs[:, None])
        & (key_places[None, :] <= query_places[:, None])
    )
    scores = (
        jnp.einsum("qhmd,khmd->hmqk", query_split, key_split, preferred_element_type=jnp.float32)
        * score_scale
    )
    scores = jnp.where(visible, scores, NEG_FILL)
    new_max = jnp.maximum(run_max, jnp.max(scores, axis=-1))
    weights = jnp.where(visible, jnp.exp(scores - new_max[..., None]), 0.0)
    totals = jnp.sum(weights, axis=-1)
    weighted = jnp.einsum(
        "hmqk,khe->hmqe",
        weights.astype(jnp.bfloat16),
        value_split,
        preferred_element_type=jnp.float32,
    )
    run_max, totals, weighted = (new_max, totals, weighted)
    map_outputs = weighted / totals[..., None]
    difference = map_outputs[:, 0] - lambda_mix * map_outputs[:, 1]
    head_outputs = rms_rows(difference) * (1.0 - LAMBDA_INIT)
    attention = (
        jnp.transpose(head_outputs, (1, 0, 2)).reshape(row_count, feat_width).astype(jnp.bfloat16)
    )
    residual_mid = (
        layer_input.astype(jnp.float32)
        + jnp.dot(attention, out_weight, preferred_element_type=jnp.float32)
    ).astype(jnp.bfloat16)
    gathered = lax.all_gather(residual_mid, "req", axis=0, tiled=True)
    normed = (rms_rows(gathered.astype(jnp.float32)) * ffn_gain).astype(jnp.bfloat16)
    gate_proj = jnp.dot(normed, gate_weight, preferred_element_type=jnp.float32)
    up_proj = jnp.dot(normed, up_weight, preferred_element_type=jnp.float32)
    hidden = (jax.nn.silu(gate_proj) * up_proj).astype(jnp.bfloat16)
    ffn_own = lax.psum_scatter(
        jnp.dot(hidden, down_weight, preferred_element_type=jnp.float32).astype(jnp.bfloat16),
        "req",
        scatter_dimension=0,
        tiled=True,
    ).astype(jnp.float32)
    layer_output = (residual_mid.astype(jnp.float32) + ffn_own).astype(jnp.bfloat16)
    next_normed = (rms_rows(layer_output.astype(jnp.float32)) * next_gain).astype(jnp.bfloat16)
    projected_cols = jnp.dot(
        lax.all_gather(next_normed, "req", axis=0, tiled=True),
        qkv_weight,
        preferred_element_type=jnp.float32,
    ).astype(jnp.bfloat16)
    projected = lax.all_to_all(projected_cols, "req", split_axis=0, concat_axis=1, tiled=True)
    q_next = projected[:, :feat_width]
    pages_dev = row_count // PAGE
    per_owner = pages_dev // peer_count
    key_values = projected[:, feat_width:].reshape(pages_dev, PAGE, 2 * feat_width)
    owner_all = page_owner[0].reshape(peer_count, pages_dev)
    slot_all = page_slot[0].reshape(peer_count, pages_dev)
    page_numbers = jnp.arange(pages_dev, dtype=jnp.int32)
    my_owners = lax.dynamic_index_in_dim(owner_all, tok_place, 0, keepdims=False)
    send_order = jnp.argsort(my_owners * pages_dev + page_numbers)
    outgoing = key_values[send_order].reshape(peer_count, per_owner, PAGE, 2 * feat_width)
    incoming = lax.all_to_all(outgoing, "tok", split_axis=0, concat_axis=0, tiled=True)
    rank_keys = jnp.where(
        owner_all == tok_place, page_numbers[None, :], pages_dev + page_numbers[None, :]
    )
    chosen_pages = jnp.argsort(rank_keys, axis=1)[:, :per_owner]
    slot_list = jnp.take_along_axis(slot_all, chosen_pages, axis=1).reshape(pages_dev)
    page_cache = (
        jnp.zeros((pages_dev, PAGE, 2 * feat_width), jnp.bfloat16)
        .at[slot_list]
        .set(incoming.reshape(pages_dev, PAGE, 2 * feat_width))
    )
    return (layer_output, q_next, page_cache)


def solution(mesh):
    in_specs = (
        P(("req", "tok"), None),
        P(("req", "tok"), None),
        P(("req", "tok"), None),
        P(("req", "tok"), None),
        P("req", None),
        P(),
        P(),
        P(),
        P(None, "req"),
        P(None, "req"),
        P("req", None),
        P(),
        P(None, "req"),
        P("req", None),
        P("req", None),
    )
    out_specs = (P(("req", "tok"), None), P(("req", "tok"), None), P(("req", "tok"), None, None))
    return jax.shard_map(body, mesh=mesh, in_specs=in_specs, out_specs=out_specs, check_vma=False)
```

profile of v0, /device:TPU:0, one launch (start us, length us, event | category | flops | bytes accessed | tf_op | source)
XLA Modules:
  0.0 369.7 jit_solution(3113207393178205079)
XLA Ops:
  7.2 0.0 copy-start
  7.2 0.0 copy-start.8
  7.2 0.0 copy-start.1
  7.2 0.0 all-gather.4.cloned.1.call-start
  7.2 2.2 copy.38
  9.4 2.0 copy.39
  11.5 2.2 pad_maximum_fusion
  13.7 0.0 all-gather.4.cloned.1.call-update
  13.7 0.0 all-gather.6.cloned.1.call-start
  13.8 2.2 reshape.141
  16.0 0.0 copy-done.8
  16.0 0.6 multiply_reduce_fusion.1
  18.0 6.5 %gather_fusion = s32[1152]{0:T(1024)S(1)} fusion(s32[2048]{0:T(1024)S(1)} %bitcast.64, s32[2048]{0:T(1024)S(1)} %pad_clamp_fusion), kind=kCustom, calls=%fused_computation | custom fusion | bytes 13824 | tf_op jit(solution)/shard_map/jit(_take)/gather | solution.py:68
  24.5 1.1 compare_and_fusion
  25.6 112.0 %all-gather.4.cloned.1.call-done = bf16[2048,4096]{0,1:T(8,128)(2,1)} async-done(((bf16[128,4096]{0,1:T(8,128)(2,1)}), bf16[2048,4096]{0,1:T(8,128)(2,1)}) %all-gather.4.cloned.1.call-update) | async-done | bytes 16777232 | tf_op jit(solution)/shard_map/all_gather | solution.py:57
  137.5 5.1 %pad_dynamic-slice_fusion.1 = (bf16[1152,2048]{0,1:T(8,128)(2,1)}, bf16[1152,2048]{0,1:T(8,128)(2,1)S(1)}) fusion(s32[]{:T(128)S(6)} %select_n.70, s32[]{:T(128)S(6)} %add.181, bf16[2048,4096]{0,1:T(8,128)(2,1)} %all-gather.4.cloned.1.call-done), kind=kLoop, calls=%fused_computation.5 | loop fusion | bytes 26214408 | tf_op jit(solution)/shard_map/slice | solution.py:64
  142.6 2.5 fusion.3
  145.1 2.3 fusion.4
  147.4 1.3 copy-done.2
  148.7 8.3 %broadcast_divide_fusion = f32[8,2,128,256]{3,2,1,0:T(8,128)S(1)} fusion(f32[8,2,128]{2,1,0:T(2,128)S(1)} %fusion.4, bf16[1152,8,256,1]{0,2,3,1:T(8,128)(2,1)} %bitcast.68, f32[8,2,1152,128]{3,2,1,0:T(8,128)} %copy-done.2, f32[8,2,128]{2,1,0:T(2,128)S(1)} %broadcast_maximum_fusion, pred[128,1152]{0,1:T(8,128)(4,1)S(1)} %compare_and_fusion), kind=kOutput, calls=%fused_computation.41 | convolution fusion | flops 1220280320 | bytes 16416768 | tf_op jit(solution)/shard_map/hmqk,khe->hmqe/dot_general | solution.py:82
  157.0 0.2 multiply_reduce_fusion
  157.2 1.1 fusion.26
  158.3 2.0 copy.44
  160.3 5.7 %fusion.13 = bf16[128,2048]{1,0:T(8,128)(2,1)} fusion(bf16[128,2048]{0,1:T(8,128)(2,1)} %bitcast.70, bf16[2048,2048]{1,0:T(8,128)(2,1)} %param.21, bf16[128,2048]{1,0:T(8,128)(2,1)} %param.15), kind=kOutput, calls=%fused_computation.25 | convolution fusion | flops 1074528256 | bytes 9961472 | tf_op jit(solution)/shard_map/dot_general | solution.py:97
  166.0 0.0 all-gather.6.cloned.1.call-update
  166.0 0.2 reduce-scatter.2.cloned.1.call-start
  166.3 33.9 %all-gather.6.cloned.1.call-done = bf16[1024,2048]{1,0:T(8,128)(2,1)} async-done(((bf16[128,2048]{1,0:T(8,128)(2,1)}), bf16[1024,2048]{1,0:T(8,128)(2,1)}) %all-gather.6.cloned.1.call-update) | async-done | bytes 4194320 | tf_op jit(solution)/shard_map/all_gather | solution.py:99
  200.1 3.2 fusion
  203.4 0.2 copy-done.4
  203.6 6.7 %fusion.15 = f32[1024,704]{0,1:T(8,128)} fusion(bf16[2048,704]{0,1:T(8,128)(2,1)} %param.23, bf16[1024,2048]{1,0:T(8,128)(2,1)S(1)} %copy-done.4, f32[2048]{0:T(1024)S(1)} %copy-done.11, f32[1024]{0:T(1024)S(1)} %add_rsqrt_fusion), kind=kOutput, calls=%fused_computation.29 | convolution fusion | flops 2961178624 | bytes 9973760 | tf_op jit(solution)/shard_map/dot_general | solution.py:101
  210.3 12.4 %convolution_convert_fusion = bf16[1024,2048]{1,0:T(8,128)(2,1)} fusion(bf16[704,2048]{1,0:T(8,128)(2,1)} %param.25, f32[1024,704]{0,1:T(8,128)} %fusion.15, bf16[2048,704]{0,1:T(8,128)(2,1)} %param.24, bf16[1024,2048]{1,0:T(8,128)(2,1)} %all-gather.6.cloned.1.call-done, f32[2048]{0:T(1024)S(1)} %copy-done.11, f32[1024]{0:T(1024)S(1)} %add_rsqrt_fusion), kind=kOutput, calls=%fused_computation.22 | convolution fusion | flops 5920391168 | bytes 17051648 | tf_op jit(solution)/shard_map/dot_general | solution.py:105
  222.7 0.0 reduce-scatter.2.cloned.1.call-update
  222.7 0.0 all-gather.8.cloned.1.call-start
  222.8 37.9 %reduce-scatter.2.cloned.1.call-done = bf16[128,2048]{1,0:T(8,128)(2,1)} async-done(((bf16[1024,2048]{1,0:T(8,128)(2,1)}), bf16[128,2048]{1,0:T(8,128)(2,1)}) %reduce-scatter.2.cloned.1.call-update) | async-done | bytes 524304 | tf_op jit(solution)/shard_map/reduce_scatter | solution.py:104
  260.6 1.5 fusion.19
  262.1 0.8 copy-done.6
  262.9 1.0 fusion.21
  263.9 0.0 all-gather.8.cloned.1.call-update
  263.9 0.0 copy-start.9
  263.9 0.0 copy-start.10
  263.9 31.2 %all-gather.8.cloned.1.call-done = bf16[1024,2048]{1,0:T(8,128)(2,1)} async-done(((bf16[128,2048]{1,0:T(8,128)(2,1)}), bf16[1024,2048]{1,0:T(8,128)(2,1)}) %all-gather.8.cloned.1.call-update) | async-done | bytes 4194320 | tf_op jit(solution)/shard_map/all_gather | solution.py:113
  295.1 6.8 %convolution_convert_fusion.1 = bf16[1024,768]{1,0:T(8,128)(2,1)} fusion(bf16[1024,2048]{1,0:T(8,128)(2,1)} %all-gather.8.cloned.1.call-done, bf16[2048,768]{1,0:T(8,128)(2,1)S(1)} %copy-done), kind=kOutput, calls=%fused_computation.26 | convolution fusion | flops 3222011904 | bytes 8912896 | tf_op jit(solution)/shard_map/dot_general | solution.py:112
  301.8 4.3 %all-to-all-start = ((bf16[8,128,768]{2,1,0:T(8,128)(2,1)}), bf16[8,128,768]{2,1,0:T(8,128)(2,1)}, u32[]{:S(2)}, u32[]{:S(2)}) async-start(bf16[8,128,768]{2,1,0:T(8,128)(2,1)} %bitcast.71), calls=%async_computation.1 | async-start | bytes 3145728 | tf_op jit(solution)/shard_map/all_to_all | solution.py:117
  306.1 0.5 broadcast.220
  306.6 0.7 reduce.11
  307.3 0.1 reshape_squeeze.6
  307.4 0.1 copy.46
  307.5 0.0 copy-done.10
  307.5 0.7 reduce.10
  308.1 0.1 reshape_squeeze.7
  308.2 1.2 sort.35
  309.5 18.2 %all-to-all-done = bf16[8,128,768]{2,1,0:T(8,128)(2,1)} async-done(((bf16[8,128,768]{2,1,0:T(8,128)(2,1)}), bf16[8,128,768]{2,1,0:T(8,128)(2,1)}, u32[]{:S(2)}, u32[]{:S(2)}) %all-to-all-start) | async-done | bytes 1572896 | tf_op jit(solution)/shard_map/all_to_all | solution.py:117
  327.7 1.6 copy.52
  329.3 1.1 copy-done.3
  330.4 1.0 slice_bitcast_fusion
  331.5 2.8 gather_fusion.1
  334.3 7.0 %all-to-all-start.1 = ((bf16[16,1,8,4096]{3,2,1,0:T(8,128)(2,1)}), bf16[16,1,8,4096]{3,2,1,0:T(8,128)(2,1)}, u32[]{:S(2)}, u32[]{:S(2)}) async-start(bf16[16,1,8,4096]{3,2,1,0:T(8,128)(2,1)} %bitcast.69), calls=%async_computation.2 | async-start | bytes 2097152 | tf_op jit(solution)/shard_map/all_to_all | solution.py:128
  341.3 0.1 iota_select_fusion
  341.4 0.7 sort.34
  342.1 0.7 gather_fusion.2
  342.8 1.9 slice.52
  344.7 14.1 %all-to-all-done.1 = bf16[16,1,8,4096]{3,2,1,0:T(8,128)(2,1)} async-done(((bf16[16,1,8,4096]{3,2,1,0:T(8,128)(2,1)}), bf16[16,1,8,4096]{3,2,1,0:T(8,128)(2,1)}, u32[]{:S(2)}, u32[]{:S(2)}) %all-to-all-start.1) | async-done | bytes 1048608 | tf_op jit(solution)/shard_map/all_to_all | solution.py:128
  358.8 1.1 broadcast_in_dim.64
  359.8 3.4 scatter_fusion
  (34 shorter events, 0.2 us)
Async XLA Ops:
  7.2 287.9 %copy-start = (bf16[2048,768]{1,0:T(8,128)(2,1)S(1)}, bf16[2048,768]{1,0:T(8,128)(2,1)}, u32[]{:S(2)}) copy-start(bf16[2048,768]{1,0:T(8,128)(2,1)} %param.27) | copy-start | bytes 9437188
  7.2 8.8 %copy-start.8 = (f32[4,128]{1,0:T(4,128)S(1)}, f32[4,128]{1,0:T(4,128)}, u32[]{:S(2)}) copy-start(f32[4,128]{1,0:T(4,128)} %param.20) | copy-start | bytes 6148
  7.2 10.8 %copy-start.1 = (s32[1,2048]{1,0:T(1,128)S(1)}, s32[1,2048]{1,0:T(1,128)}, u32[]{:S(2)}) copy-start(s32[1,2048]{1,0:T(1,128)} %param.19) | copy-start | bytes 24580
  7.2 130.3 %all-gather.4.cloned.1.call-start = ((), (), s32[]{:S(2)}) async-start(), calls=%async_computation.3 | async-start | bytes 17825792 | tf_op jit(solution)/shard_map/all_gather | solution.py:57
  13.7 186.4 %all-gather.6.cloned.1.call-start = ((), (), s32[]{:S(2)}) async-start(), calls=%async_computation.4 | async-start | bytes 4718592 | tf_op jit(solution)/shard_map/all_gather | solution.py:99
  137.5 5.1 %copy-start.5 = (bf16[128,8,2,128]{3,2,1,0:T(2,128)(2,1)S(1)}, bf16[128,8,2,128]{3,2,1,0:T(2,128)(2,1)}, u32[]{:S(2)}) copy-start(bf16[128,8,2,128]{3,2,1,0:T(2,128)(2,1)} %reshape.141) | copy-start | bytes 1572868
  145.1 3.6 copy-start.2
  166.0 37.4 %copy-start.11 = (f32[2048]{0:T(1024)S(1)}, f32[2048]{0:T(1024)}, u32[]{:S(2)}) copy-start(f32[2048]{0:T(1024)} %param.22) | copy-start | bytes 24580
  166.0 94.6 %reduce-scatter.2.cloned.1.call-start = ((), (), s32[]{:S(2)}) async-start(), calls=%async_computation.5 | async-start | bytes 4718592 | tf_op jit(solution)/shard_map/reduce_scatter | solution.py:104
  200.1 3.4 copy-start.4
  222.7 40.2 %copy-start.7 = (f32[2048]{0:T(1024)S(1)}, f32[2048]{0:T(1024)}, u32[]{:S(2)}) copy-start(f32[2048]{0:T(1024)} %param.26) | copy-start | bytes 24580
  222.7 72.4 %all-gather.8.cloned.1.call-start = ((), (), s32[]{:S(2)}) async-start(), calls=%async_computation.6 | async-start | bytes 4718592 | tf_op jit(solution)/shard_map/all_gather | solution.py:113
  262.1 0.8 copy-start.6
  263.9 42.8 %copy-start.9 = (s32[1,256]{1,0:T(1,128)S(1)}, s32[1,256]{1,0:T(1,128)}, u32[]{:S(2)}) copy-start(s32[1,256]{1,0:T(1,128)} %param.28) | copy-start | bytes 3076
  263.9 43.6 %copy-start.10 = (s32[1,256]{1,0:T(1,128)S(1)}, s32[1,256]{1,0:T(1,128)}, u32[]{:S(2)}) copy-start(s32[1,256]{1,0:T(1,128)} %param.29) | copy-start | bytes 3076
  301.8 25.9 %all-to-all-start = ((bf16[8,128,768]{2,1,0:T(8,128)(2,1)}), bf16[8,128,768]{2,1,0:T(8,128)(2,1)}, u32[]{:S(2)}, u32[]{:S(2)}) async-start(bf16[8,128,768]{2,1,0:T(8,128)(2,1)} %bitcast.71), calls=%async_computation.1 | async-start | bytes 3145728 | tf_op jit(solution)/shard_map/all_to_all | solution.py:117
  329.3 1.2 copy-start.3
  334.3 24.4 %all-to-all-start.1 = ((bf16[16,1,8,4096]{3,2,1,0:T(8,128)(2,1)}), bf16[16,1,8,4096]{3,2,1,0:T(8,128)(2,1)}, u32[]{:S(2)}, u32[]{:S(2)}) async-start(bf16[16,1,8,4096]{3,2,1,0:T(8,128)(2,1)} %bitcast.69), calls=%async_computation.2 | async-start | bytes 2097152 | tf_op jit(solution)/shard_map/all_to_all | solution.py:128
Sparse Core Ops, SparseCore 0:
  13.9 123.6 all-gather.3
  166.1 33.9 all-gather.5
  222.8 37.7 reduce-scatter.1
  264.0 31.0 all-gather.7
where the time goes:
time: 370 us
  waiting for transfers between devices  247 us (67%)
  matrix products  42.3 us (11%)
  local copies, waits for them, and re-layouts  36.7 us (10%)
  other arithmetic  16.7 us (5%)
  between operations  15.3 us (4%)
  starting transfers between devices  11.6 us (3%)
    all_gather x1, waiting for transfers between devices, body(): all_kv = lax.all_gather(own_kv, 'tok', axis=0, tiled=True)  112 us
    reduce_scatter x1, waiting for transfers between devices, body(): lax.psum_scatter(jnp.dot(hidden, down_weight, preferred_element_type=jnp....  37.9 us
    all_gather x1, waiting for transfers between devices, body(): gathered = lax.all_gather(residual_mid, 'req', axis=0, tiled=True)  33.9 us
    all_gather x1, waiting for transfers between devices, body(): lax.all_gather(next_normed, 'req', axis=0, tiled=True)  31.2 us
    all_to_all x1, waiting for transfers between devices, body(): lax.all_to_all(projected_cols, 'req', split_axis=0, concat_axis=1, tiled=...  18.2 us
    all_to_all x1, waiting for transfers between devices, body(): lax.all_to_all(outgoing, 'tok', split_axis=0, concat_axis=0, tiled=True)  14.1 us
    dot_general x1, matrix products, body(): jnp.dot(hidden, down_weight, preferred_element_type=jnp.float32)  12.4 us
    dot_general x1, matrix products, body(): jnp.einsum('hmqk,khe->hmqe', weights.astype(jnp.bfloat16), value_split, p...  8.27 us
  transfers between devices with their start and end apart: 6, of which 6 were waited for; matrix products, arithmetic and copies ran while one was open for 5% of the time, Pallas kernels for 0%

commit v1 on v0

--- a/solution.py
+++ b/solution.py
@@ -54,7 +54,23 @@
     run_max = jnp.full((HEADS, 2, row_count), NEG_FILL, jnp.float32)
     back = -(-(MAX_SEG - 1) // row_count)
     own_kv = jnp.concatenate([k_in, v_in], axis=1)
-    all_kv = lax.all_gather(own_kv, "tok", axis=0, tiled=True)
+    size, index, width = (lax.axis_size("tok"), lax.axis_index("tok"), own_kv.shape[0])
+    forward = [(i, (i + 1) % size) for i in range(size)]
+    left = [(i, (i - 1) % size) for i in range(size)]
+    all_kv = jnp.zeros((*own_kv.shape[:0], size * width, *own_kv.shape[0 + 1 :]), own_kv.dtype)
+    all_kv = lax.dynamic_update_slice_in_dim(all_kv, own_kv, index * width, axis=0)
+    from_left = from_right = own_kv
+    half = size // 2
+    for step in range(1, half + 1):
+        from_left = lax.ppermute(from_left, "tok", forward)
+        all_kv = lax.dynamic_update_slice_in_dim(
+            all_kv, from_left, (index - step) % size * width, axis=0
+        )
+        if step < size - half:
+            from_right = lax.ppermute(from_right, "tok", left)
+            all_kv = lax.dynamic_update_slice_in_dim(
+                all_kv, from_right, (index + step) % size * width, axis=0
+            )
     padded_kv = jnp.concatenate(
         [jnp.zeros((back * row_count, 2 * feat_width), all_kv.dtype), all_kv], axis=0
     )

time: 370 us -> 458 us (1.24)
  starting transfers between devices: 11.6 us -> 51.7 us
  local copies, waits for them, and re-layouts: 36.7 us -> 70.2 us
  waiting for transfers between devices: 247 us -> 260 us
    ppermute x0 -> x15, waiting for transfers between devices: none -> 129 us  [the longest x8 122 us: body(): from_left = lax.ppermute(from_left, 'tok', forward)]
    all_gather x1 -> x0, waiting for transfers between devices: 112 us -> none  [body(): all_kv = lax.all_gather(own_kv, 'tok', axis=0, tiled=True)]
    ppermute x0 -> x15, starting transfers between devices: none -> 40 us  [the longest x7 38 us: body(): from_right = lax.ppermute(from_right, 'tok', left)]
    dynamic_update_slice x0 -> x15, local copies, waits for them, and re-layouts: none -> 25.4 us  [the longest x8 13.9 us: body(): lax.dynamic_update_slice_in_dim(all_kv, from_left, (index - step) % size...]
    broadcast_in_dim x0 -> x1, local copies, waits for them, and re-layouts: none -> 5.97 us  [body(): jnp.zeros((*own_kv.shape[:0], size * width, *own_kv.shape[0 + 1:]), own_k...]
    unnamed x28 -> x30, local copies, waits for them, and re-layouts: 8.25 us -> 10.3 us
  transfers between devices with their start and end apart: 6 -> 20, of which waited for: 6 -> 18; matrix products, arithmetic and copies ran while one was open for 5% -> 9% of each run, Pallas kernels for 0% -> 0%
where the time goes in v1:
time: 458 us; the launch traced here: 457 us
  waiting for transfers between devices  260 us (57%)
  local copies, waits for them, and re-layouts  70.2 us (15%)
  starting transfers between devices  51.7 us (11%)
  matrix products  43.6 us (10%)
  between operations  15.6 us (3%)
  other arithmetic  15.4 us (3%)
    ppermute x8, waiting for transfers between devices, body(): from_left = lax.ppermute(from_left, 'tok', forward)  122 us
    ppermute x7, starting transfers between devices, body(): from_right = lax.ppermute(from_right, 'tok', left)  38 us
    reduce_scatter x1, waiting for transfers between devices, body(): lax.psum_scatter(jnp.dot(hidden, down_weight, preferred_element_type=jnp....  37.9 us
    all_gather x1, waiting for transfers between devices, body(): lax.all_gather(next_normed, 'req', axis=0, tiled=True)  31.2 us
    all_gather x1, waiting for transfers between devices, body(): gathered = lax.all_gather(residual_mid, 'req', axis=0, tiled=True)  30 us
    all_to_all x1, waiting for transfers between devices, body(): lax.all_to_all(projected_cols, 'req', split_axis=0, concat_axis=1, tiled=...  18.2 us
    all_to_all x1, waiting for transfers between devices, body(): lax.all_to_all(outgoing, 'tok', split_axis=0, concat_axis=0, tiled=True)  14.1 us
    dynamic_update_slice x8, local copies, waits for them, and re-layouts, body(): lax.dynamic_update_slice_in_dim(all_kv, from_left, (index - step) % size...  13.9 us
  transfers between devices with their start and end apart: 20, of which 18 were waited for; matrix products, arithmetic and copies ran while one was open for 9% of the time, Pallas kernels for 0%

profile of v1, /device:TPU:0, one launch (start us, length us, event | category | flops | bytes accessed | tf_op | source)
XLA Modules:
  0.0 456.8 jit_solution(4919232238997511249)
XLA Ops:
  7.2 2.2 copy.38
  9.4 2.0 copy.39
  11.5 6.0 %broadcast_in_dim.64 = bf16[2048,4096]{0,1:T(8,128)(2,1)} broadcast(bf16[]{:T(256)} %constant.151.clone.1), dimensions={} | broadcast | bytes 16777218 | tf_op jit(solution)/shard_map/broadcast_in_dim | solution.py:60
  17.5 1.2 pad_maximum_fusion
  18.7 2.0 collective-permute-start
  20.7 4.3 collective-permute-start.1
  25.0 23.3 %collective-permute-done = bf16[128,4096]{0,1:T(8,128)(2,1)} collective-permute-done((bf16[128,4096]{0,1:T(8,128)(2,1)S(1)}, bf16[128,4096]{0,1:T(8,128)(2,1)}, u32[]{:S(2)}, u32[]{:S(2)}) %collective-permute-start) | collective-permute-done | bytes 1048608 | tf_op jit(solution)/shard_map/ppermute | solution.py:65
  48.2 5.3 %collective-permute-start.3 = (bf16[128,4096]{0,1:T(8,128)(2,1)}, bf16[128,4096]{0,1:T(8,128)(2,1)}, u32[]{:S(2)}, u32[]{:S(2)}) collective-permute-start(bf16[128,4096]{0,1:T(8,128)(2,1)} %collective-permute-done.1), channel_id=1, source_target_pairs={{0,15},{1,0},{2,1},{3,2},{4,3},{5,4},{6,5},{7,6},{8,7},{9,8},{10,9... | collective-permute-start | bytes 3145736 | tf_op jit(solution)/shard_map/ppermute | solution.py:70
  53.6 22.6 %collective-permute-done.2 = bf16[128,4096]{0,1:T(8,128)(2,1)} collective-permute-done((bf16[128,4096]{0,1:T(8,128)(2,1)}, bf16[128,4096]{0,1:T(8,128)(2,1)}, u32[]{:S(2)}, u32[]{:S(2)}) %collective-permute-start.2) | collective-permute-done | bytes 1048608 | tf_op jit(solution)/shard_map/ppermute | solution.py:65
  76.4 6.5 %gather_fusion = s32[1152]{0:T(1024)S(1)} fusion(s32[2048]{0:T(1024)S(1)} %bitcast.64, s32[2048]{0:T(1024)S(1)} %pad_clamp_fusion), kind=kCustom, calls=%fused_computation | custom fusion | bytes 13824 | tf_op jit(solution)/shard_map/jit(_take)/gather | solution.py:84
  82.9 5.3 %collective-permute-start.5 = (bf16[128,4096]{0,1:T(8,128)(2,1)}, bf16[128,4096]{0,1:T(8,128)(2,1)}, u32[]{:S(2)}, u32[]{:S(2)}) collective-permute-start(bf16[128,4096]{0,1:T(8,128)(2,1)} %collective-permute-done.3), channel_id=1, source_target_pairs={{0,15},{1,0},{2,1},{3,2},{4,3},{5,4},{6,5},{7,6},{8,7},{9,8},{10,9... | collective-permute-start | bytes 3145736 | tf_op jit(solution)/shard_map/ppermute | solution.py:70
  88.2 2.2 reshape.141
  91.4 11.8 %collective-permute-done.4 = bf16[128,4096]{0,1:T(8,128)(2,1)} collective-permute-done((bf16[128,4096]{0,1:T(8,128)(2,1)}, bf16[128,4096]{0,1:T(8,128)(2,1)}, u32[]{:S(2)}, u32[]{:S(2)}) %collective-permute-start.4) | collective-permute-done | bytes 1048608 | tf_op jit(solution)/shard_map/ppermute | solution.py:65
  105.3 2.4 constant_dynamic-update-slice_fusion.14
  107.7 1.5 collective-permute-done.5
  109.2 5.8 %collective-permute-start.7 = (bf16[128,4096]{0,1:T(8,128)(2,1)}, bf16[128,4096]{0,1:T(8,128)(2,1)S(1)}, u32[]{:S(2)}, u32[]{:S(2)}) collective-permute-start(bf16[128,4096]{0,1:T(8,128)(2,1)} %collective-permute-done.5), channel_id=1, source_target_pairs={{0,15},{1,0},{2,1},{3,2},{4,3},{5,4},{6,5},{7,6},{8,7},{9,8},{10,9... | collective-permute-start | bytes 3145736 | tf_op jit(solution)/shard_map/ppermute | solution.py:70
  115.0 2.4 constant_dynamic-update-slice_fusion.13
  117.3 12.1 %collective-permute-done.6 = bf16[128,4096]{0,1:T(8,128)(2,1)} collective-permute-done((bf16[128,4096]{0,1:T(8,128)(2,1)}, bf16[128,4096]{0,1:T(8,128)(2,1)}, u32[]{:S(2)}, u32[]{:S(2)}) %collective-permute-start.6) | collective-permute-done | bytes 1048608 | tf_op jit(solution)/shard_map/ppermute | solution.py:65
  129.4 2.3 constant_dynamic-update-slice_fusion.12
  131.7 2.4 constant_dynamic-update-slice_fusion.11
  135.0 5.7 %collective-permute-start.9 = (bf16[128,4096]{0,1:T(8,128)(2,1)S(1)}, bf16[128,4096]{0,1:T(8,128)(2,1)S(1)}, u32[]{:S(2)}, u32[]{:S(2)}) collective-permute-start(bf16[128,4096]{0,1:T(8,128)(2,1)S(1)} %collective-permute-done.7), channel_id=1, source_target_pairs={{0,15},{1,0},{2,1},{3,2},{4,3},{5,4},{6,5},{7,6},{8,7},{9,8},{10,9... | collective-permute-start | bytes 3145736 | tf_op jit(solution)/shard_map/ppermute | solution.py:70
  140.7 2.3 constant_dynamic-update-slice_fusion.10
  143.1 11.5 %collective-permute-done.8 = bf16[128,4096]{0,1:T(8,128)(2,1)S(1)} collective-permute-done((bf16[128,4096]{0,1:T(8,128)(2,1)}, bf16[128,4096]{0,1:T(8,128)(2,1)S(1)}, u32[]{:S(2)}, u32[]{:S(2)}) %collective-permute-start.8) | collective-permute-done | bytes 1048608 | tf_op jit(solution)/shard_map/ppermute | solution.py:65
  154.5 2.3 constant_dynamic-update-slice_fusion.9
  156.8 2.4 constant_dynamic-update-slice_fusion.8
  159.5 5.8 %collective-permute-start.11 = (bf16[128,4096]{0,1:T(8,128)(2,1)S(1)}, bf16[128,4096]{0,1:T(8,128)(2,1)S(1)}, u32[]{:S(2)}, u32[]{:S(2)}) collective-permute-start(bf16[128,4096]{0,1:T(8,128)(2,1)S(1)} %collective-permute-done.9), channel_id=1, source_target_pairs={{0,15},{1,0},{2,1},{3,2},{4,3},{5,4},{6,5},{7,6},{8,7},{9,8},{10,9... | collective-permute-start | bytes 3145736 | tf_op jit(solution)/shard_map/ppermute | solution.py:70
  165.3 1.1 constant_dynamic-update-slice_fusion.7
  166.5 12.0 %collective-permute-done.10 = bf16[128,4096]{0,1:T(8,128)(2,1)S(1)} collective-permute-done((bf16[128,4096]{0,1:T(8,128)(2,1)S(1)}, bf16[128,4096]{0,1:T(8,128)(2,1)S(1)}, u32[]{:S(2)}, u32[]{:S(2)}) %collective-permute-start.10) | collective-permute-done | bytes 1048608 | tf_op jit(solution)/shard_map/ppermute | solution.py:65
  178.5 1.1 constant_dynamic-update-slice_fusion.6
  179.6 1.1 constant_dynamic-update-slice_fusion.5
  180.7 2.5 collective-permute-done.11
  183.2 5.8 %collective-permute-start.13 = (bf16[128,4096]{0,1:T(8,128)(2,1)S(1)}, bf16[128,4096]{0,1:T(8,128)(2,1)S(1)}, u32[]{:S(2)}, u32[]{:S(2)}) collective-permute-start(bf16[128,4096]{0,1:T(8,128)(2,1)S(1)} %collective-permute-done.11), channel_id=1, source_target_pairs={{0,15},{1,0},{2,1},{3,2},{4,3},{5,4},{6,5},{7,6},{8,7},{9,8},{10,9... | collective-permute-start | bytes 3145736 | tf_op jit(solution)/shard_map/ppermute | solution.py:70
  189.0 1.1 constant_dynamic-update-slice_fusion.4
  190.2 11.7 %collective-permute-done.12 = bf16[128,4096]{0,1:T(8,128)(2,1)S(1)} collective-permute-done((bf16[128,4096]{0,1:T(8,128)(2,1)S(1)}, bf16[128,4096]{0,1:T(8,128)(2,1)S(1)}, u32[]{:S(2)}, u32[]{:S(2)}) %collective-permute-start.12) | collective-permute-done | bytes 1048608 | tf_op jit(solution)/shard_map/ppermute | solution.py:65
  201.8 1.1 constant_dynamic-update-slice_fusion.3
  202.9 1.2 constant_dynamic-update-slice_fusion.2
  204.1 1.9 collective-permute-done.13
  207.1 16.9 %collective-permute-done.14 = bf16[128,4096]{0,1:T(8,128)(2,1)S(1)} collective-permute-done((bf16[128,4096]{0,1:T(8,128)(2,1)S(1)}, bf16[128,4096]{0,1:T(8,128)(2,1)S(1)}, u32[]{:S(2)}, u32[]{:S(2)}) %collective-permute-start.14) | collective-permute-done | bytes 1048608 | tf_op jit(solution)/shard_map/ppermute | solution.py:65
  224.0 1.1 constant_dynamic-update-slice_fusion
  225.1 5.1 %pad_dynamic-slice_fusion.1 = (bf16[1152,2048]{0,1:T(8,128)(2,1)}, bf16[1152,2048]{0,1:T(8,128)(2,1)S(1)}) fusion(s32[]{:T(128)S(6)} %select_n.209, s32[]{:T(128)S(6)} %add.338, bf16[2048,4096]{0,1:T(8,128)(2,1)} %constant_dynamic-update-slice_fusion), kind=kLoop, calls=%fused_computation.5 | loop fusion | bytes 26214408 | tf_op jit(solution)/shard_map/slice | solution.py:80
  230.2 2.5 fusion.3
  232.7 3.6 copy-done.2
  236.3 2.3 fusion.4
  238.6 8.3 %broadcast_divide_fusion = f32[8,2,128,256]{3,2,1,0:T(8,128)S(1)} fusion(f32[8,2,128]{2,1,0:T(2,128)S(1)} %fusion.4, bf16[1152,8,256,1]{0,2,3,1:T(8,128)(2,1)} %bitcast.68, f32[8,2,1152,128]{3,2,1,0:T(8,128)} %copy-done.2, f32[8,2,128]{2,1,0:T(2,128)S(1)} %broadcast_maximum_fusion, pred[128,1152]{0,1:T(8,128)(4,1)S(1)} %compare_and_fusion), kind=kOutput, calls=%fused_computation.41 | convolution fusion | flops 1220280320 | bytes 16416768 | tf_op jit(solution)/shard_map/hmqk,khe->hmqe/dot_general | solution.py:98
  248.2 2.0 copy.44
  250.3 5.7 %fusion.13 = bf16[128,2048]{1,0:T(8,128)(2,1)} fusion(bf16[128,2048]{0,1:T(8,128)(2,1)} %bitcast.70, bf16[2048,2048]{1,0:T(8,128)(2,1)} %param.21, bf16[128,2048]{1,0:T(8,128)(2,1)} %param.15), kind=kOutput, calls=%fused_computation.25 | convolution fusion | flops 1074528256 | bytes 9961472 | tf_op jit(solution)/shard_map/dot_general | solution.py:113
  256.2 30.0 %all-gather.3.cloned.1.call-done = bf16[1024,2048]{1,0:T(8,128)(2,1)} async-done(((bf16[128,2048]{1,0:T(8,128)(2,1)}), bf16[1024,2048]{1,0:T(8,128)(2,1)}) %all-gather.3.cloned.1.call-update) | async-done | bytes 4194320 | tf_op jit(solution)/shard_map/all_gather | solution.py:115
  286.2 3.1 fusion
  289.3 8.0 %fusion.15 = f32[1024,704]{0,1:T(8,128)} fusion(bf16[2048,704]{0,1:T(8,128)(2,1)} %param.23, bf16[1024,2048]{1,0:T(8,128)(2,1)} %all-gather.3.cloned.1.call-done, f32[2048]{0:T(1024)S(1)} %copy-done.12, f32[1024]{0:T(1024)S(1)} %add_rsqrt_fusion), kind=kOutput, calls=%fused_computation.29 | convolution fusion | flops 2961178624 | bytes 9973760 | tf_op jit(solution)/shard_map/dot_general | solution.py:117
  297.3 12.4 %convolution_convert_fusion = bf16[1024,2048]{1,0:T(8,128)(2,1)} fusion(bf16[704,2048]{1,0:T(8,128)(2,1)} %param.25, f32[1024,704]{0,1:T(8,128)} %fusion.15, bf16[2048,704]{0,1:T(8,128)(2,1)} %param.24, bf16[1024,2048]{1,0:T(8,128)(2,1)} %all-gather.3.cloned.1.call-done, f32[2048]{0:T(1024)S(1)} %copy-done.12, f32[1024]{0:T(1024)S(1)} %add_rsqrt_fusion), kind=kOutput, calls=%fused_computation.22 | convolution fusion | flops 5920391168 | bytes 17051648 | tf_op jit(solution)/shard_map/dot_general | solution.py:121
  309.8 37.9 %reduce-scatter.2.cloned.1.call-done = bf16[128,2048]{1,0:T(8,128)(2,1)} async-done(((bf16[1024,2048]{1,0:T(8,128)(2,1)}), bf16[128,2048]{1,0:T(8,128)(2,1)}) %reduce-scatter.2.cloned.1.call-update) | async-done | bytes 524304 | tf_op jit(solution)/shard_map/reduce_scatter | solution.py:120
  347.6 1.5 fusion.19
  350.9 31.2 %all-gather.5.cloned.1.call-done = bf16[1024,2048]{1,0:T(8,128)(2,1)} async-done(((bf16[128,2048]{1,0:T(8,128)(2,1)}), bf16[1024,2048]{1,0:T(8,128)(2,1)}) %all-gather.5.cloned.1.call-update) | async-done | bytes 4194320 | tf_op jit(solution)/shard_map/all_gather | solution.py:129
  382.1 6.8 %convolution_convert_fusion.1 = bf16[1024,768]{1,0:T(8,128)(2,1)} fusion(bf16[1024,2048]{1,0:T(8,128)(2,1)} %all-gather.5.cloned.1.call-done, bf16[2048,768]{1,0:T(8,128)(2,1)S(1)} %copy-done), kind=kOutput, calls=%fused_computation.26 | convolution fusion | flops 3222011904 | bytes 8912896 | tf_op jit(solution)/shard_map/dot_general | solution.py:128
  388.9 4.3 all-to-all-start
  395.3 1.2 sort.35
  396.6 18.2 %all-to-all-done = bf16[8,128,768]{2,1,0:T(8,128)(2,1)} async-done(((bf16[8,128,768]{2,1,0:T(8,128)(2,1)}), bf16[8,128,768]{2,1,0:T(8,128)(2,1)}, u32[]{:S(2)}, u32[]{:S(2)}) %all-to-all-start) | async-done | bytes 1572896 | tf_op jit(solution)/shard_map/all_to_all | solution.py:133
  414.8 1.6 copy.52
  416.4 1.1 copy-done.3
  418.5 2.8 gather_fusion.1
  421.4 7.0 %all-to-all-start.1 = ((bf16[16,1,8,4096]{3,2,1,0:T(8,128)(2,1)}), bf16[16,1,8,4096]{3,2,1,0:T(8,128)(2,1)}, u32[]{:S(2)}, u32[]{:S(2)}) async-start(bf16[16,1,8,4096]{3,2,1,0:T(8,128)(2,1)} %bitcast.69), calls=%async_computation.2 | async-start | bytes 2097152 | tf_op jit(solution)/shard_map/all_to_all | solution.py:144
  429.9 1.9 slice.52
  431.7 14.1 %all-to-all-done.1 = bf16[16,1,8,4096]{3,2,1,0:T(8,128)(2,1)} async-done(((bf16[16,1,8,4096]{3,2,1,0:T(8,128)(2,1)}), bf16[16,1,8,4096]{3,2,1,0:T(8,128)(2,1)}, u32[]{:S(2)}, u32[]{:S(2)}) %all-to-all-start.1) | async-done | bytes 1048608 | tf_op jit(solution)/shard_map/all_to_all | solution.py:144
  446.9 3.4 scatter_fusion
  (79 shorter events, 13.3 us)
Async XLA Ops:
  7.2 375.0 %copy-start = (bf16[2048,768]{1,0:T(8,128)(2,1)S(1)}, bf16[2048,768]{1,0:T(8,128)(2,1)}, u32[]{:S(2)}) copy-start(bf16[2048,768]{1,0:T(8,128)(2,1)} %param.27) | copy-start | bytes 9437188
  7.2 279.0 %all-gather.3.cloned.1.call-start = ((), (), s32[]{:S(2)}) async-start(), calls=%async_computation.3 | async-start | bytes 4718592 | tf_op jit(solution)/shard_map/all_gather | solution.py:115
  11.5 6.0 %copy-start.6 = (bf16[128,2048]{0,1:T(8,128)(2,1)S(1)}, bf16[128,2048]{0,1:T(8,128)(2,1)}, u32[]{:S(2)}) copy-start(bf16[128,2048]{0,1:T(8,128)(2,1)} %copy.38) | copy-start | bytes 1572868
  11.5 6.0 %copy-start.7 = (bf16[128,2048]{0,1:T(8,128)(2,1)S(1)}, bf16[128,2048]{0,1:T(8,128)(2,1)}, u32[]{:S(2)}) copy-start(bf16[128,2048]{0,1:T(8,128)(2,1)} %copy.39) | copy-start | bytes 1572868
  11.5 64.9 %copy-start.1 = (s32[1,2048]{1,0:T(1,128)S(1)}, s32[1,2048]{1,0:T(1,128)}, u32[]{:S(2)}) copy-start(s32[1,2048]{1,0:T(1,128)} %param.19) | copy-start | bytes 24580
  17.4 85.8 %copy-start.9 = (f32[4,128]{1,0:T(4,128)S(1)}, f32[4,128]{1,0:T(4,128)}, u32[]{:S(2)}) copy-start(f32[4,128]{1,0:T(4,128)} %param.20) | copy-start | bytes 6148
  18.7 29.6 %collective-permute-start = (bf16[128,4096]{0,1:T(8,128)(2,1)S(1)}, bf16[128,4096]{0,1:T(8,128)(2,1)}, u32[]{:S(2)}, u32[]{:S(2)}) collective-permute-start(bf16[128,4096]{0,1:T(8,128)(2,1)S(1)} %get-tuple-element.13), channel_id=1, source_target_pairs={{0,1},{1,2},{2,3},{3,4},{4,5},{5,6},{6,7},{7,8},{8,9},{9,10},{10,1... | collective-permute-start | bytes 3145736 | tf_op jit(solution)/shard_map/ppermute | solution.py:65
  20.7 27.6 %collective-permute-start.1 = (bf16[128,4096]{0,1:T(8,128)(2,1)S(1)}, bf16[128,4096]{0,1:T(8,128)(2,1)}, u32[]{:S(2)}, u32[]{:S(2)}) collective-permute-start(bf16[128,4096]{0,1:T(8,128)(2,1)S(1)} %get-tuple-element.13), channel_id=1, source_target_pairs={{0,15},{1,0},{2,1},{3,2},{4,3},{5,4},{6,5},{7,6},{8,7},{9,8},{10,9... | collective-permute-start | bytes 3145736 | tf_op jit(solution)/shard_map/ppermute | solution.py:70
  48.2 28.0 %collective-permute-start.2 = (bf16[128,4096]{0,1:T(8,128)(2,1)}, bf16[128,4096]{0,1:T(8,128)(2,1)}, u32[]{:S(2)}, u32[]{:S(2)}) collective-permute-start(bf16[128,4096]{0,1:T(8,128)(2,1)} %collective-permute-done), channel_id=1, source_target_pairs={{0,1},{1,2},{2,3},{3,4},{4,5},{5,6},{6,7},{7,8},{8,9},{9,10},{10,1... | collective-permute-start | bytes 3145736 | tf_op jit(solution)/shard_map/ppermute | solution.py:65
  48.2 34.7 %collective-permute-start.3 = (bf16[128,4096]{0,1:T(8,128)(2,1)}, bf16[128,4096]{0,1:T(8,128)(2,1)}, u32[]{:S(2)}, u32[]{:S(2)}) collective-permute-start(bf16[128,4096]{0,1:T(8,128)(2,1)} %collective-permute-done.1), channel_id=1, source_target_pairs={{0,15},{1,0},{2,1},{3,2},{4,3},{5,4},{6,5},{7,6},{8,7},{9,8},{10,9... | collective-permute-start | bytes 3145736 | tf_op jit(solution)/shard_map/ppermute | solution.py:70
  76.2 27.1 %collective-permute-start.4 = (bf16[128,4096]{0,1:T(8,128)(2,1)}, bf16[128,4096]{0,1:T(8,128)(2,1)}, u32[]{:S(2)}, u32[]{:S(2)}) collective-permute-start(bf16[128,4096]{0,1:T(8,128)(2,1)} %collective-permute-done.2), channel_id=1, source_target_pairs={{0,1},{1,2},{2,3},{3,4},{4,5},{5,6},{6,7},{7,8},{8,9},{9,10},{10,1... | collective-permute-start | bytes 3145736 | tf_op jit(solution)/shard_map/ppermute | solution.py:65
  82.9 26.2 %collective-permute-start.5 = (bf16[128,4096]{0,1:T(8,128)(2,1)}, bf16[128,4096]{0,1:T(8,128)(2,1)}, u32[]{:S(2)}, u32[]{:S(2)}) collective-permute-start(bf16[128,4096]{0,1:T(8,128)(2,1)} %collective-permute-done.3), channel_id=1, source_target_pairs={{0,15},{1,0},{2,1},{3,2},{4,3},{5,4},{6,5},{7,6},{8,7},{9,8},{10,9... | collective-permute-start | bytes 3145736 | tf_op jit(solution)/shard_map/ppermute | solution.py:70
  103.3 26.1 %collective-permute-start.6 = (bf16[128,4096]{0,1:T(8,128)(2,1)}, bf16[128,4096]{0,1:T(8,128)(2,1)}, u32[]{:S(2)}, u32[]{:S(2)}) collective-permute-start(bf16[128,4096]{0,1:T(8,128)(2,1)} %collective-permute-done.4), channel_id=1, source_target_pairs={{0,1},{1,2},{2,3},{3,4},{4,5},{5,6},{6,7},{7,8},{8,9},{9,10},{10,1... | collective-permute-start | bytes 3145736 | tf_op jit(solution)/shard_map/ppermute | solution.py:65
  109.2 25.9 %collective-permute-start.7 = (bf16[128,4096]{0,1:T(8,128)(2,1)}, bf16[128,4096]{0,1:T(8,128)(2,1)S(1)}, u32[]{:S(2)}, u32[]{:S(2)}) collective-permute-start(bf16[128,4096]{0,1:T(8,128)(2,1)} %collective-permute-done.5), channel_id=1, source_target_pairs={{0,15},{1,0},{2,1},{3,2},{4,3},{5,4},{6,5},{7,6},{8,7},{9,8},{10,9... | collective-permute-start | bytes 3145736 | tf_op jit(solution)/shard_map/ppermute | solution.py:70
  129.4 25.1 %collective-permute-start.8 = (bf16[128,4096]{0,1:T(8,128)(2,1)}, bf16[128,4096]{0,1:T(8,128)(2,1)S(1)}, u32[]{:S(2)}, u32[]{:S(2)}) collective-permute-start(bf16[128,4096]{0,1:T(8,128)(2,1)} %collective-permute-done.6), channel_id=1, source_target_pairs={{0,1},{1,2},{2,3},{3,4},{4,5},{5,6},{6,7},{7,8},{8,9},{9,10},{10,1... | collective-permute-start | bytes 3145736 | tf_op jit(solution)/shard_map/ppermute | solution.py:65
  135.0 24.5 %collective-permute-start.9 = (bf16[128,4096]{0,1:T(8,128)(2,1)S(1)}, bf16[128,4096]{0,1:T(8,128)(2,1)S(1)}, u32[]{:S(2)}, u32[]{:S(2)}) collective-permute-start(bf16[128,4096]{0,1:T(8,128)(2,1)S(1)} %collective-permute-done.7), channel_id=1, source_target_pairs={{0,15},{1,0},{2,1},{3,2},{4,3},{5,4},{6,5},{7,6},{8,7},{9,8},{10,9... | collective-permute-start | bytes 3145736 | tf_op jit(solution)/shard_map/ppermute | solution.py:70
  154.5 24.0 %collective-permute-start.10 = (bf16[128,4096]{0,1:T(8,128)(2,1)S(1)}, bf16[128,4096]{0,1:T(8,128)(2,1)S(1)}, u32[]{:S(2)}, u32[]{:S(2)}) collective-permute-start(bf16[128,4096]{0,1:T(8,128)(2,1)S(1)} %collective-permute-done.8), channel_id=1, source_target_pairs={{0,1},{1,2},{2,3},{3,4},{4,5},{5,6},{6,7},{7,8},{8,9},{9,10},{10,1... | collective-permute-start | bytes 3145736 | tf_op jit(solution)/shard_map/ppermute | solution.py:65
  159.5 23.7 %collective-permute-start.11 = (bf16[128,4096]{0,1:T(8,128)(2,1)S(1)}, bf16[128,4096]{0,1:T(8,128)(2,1)S(1)}, u32[]{:S(2)}, u32[]{:S(2)}) collective-permute-start(bf16[128,4096]{0,1:T(8,128)(2,1)S(1)} %collective-permute-done.9), channel_id=1, source_target_pairs={{0,15},{1,0},{2,1},{3,2},{4,3},{5,4},{6,5},{7,6},{8,7},{9,8},{10,9... | collective-permute-start | bytes 3145736 | tf_op jit(solution)/shard_map/ppermute | solution.py:70
  178.5 23.3 %collective-permute-start.12 = (bf16[128,4096]{0,1:T(8,128)(2,1)S(1)}, bf16[128,4096]{0,1:T(8,128)(2,1)S(1)}, u32[]{:S(2)}, u32[]{:S(2)}) collective-permute-start(bf16[128,4096]{0,1:T(8,128)(2,1)S(1)} %collective-permute-done.10), channel_id=1, source_target_pairs={{0,1},{1,2},{2,3},{3,4},{4,5},{5,6},{6,7},{7,8},{8,9},{9,10},{10,1... | collective-permute-start | bytes 3145736 | tf_op jit(solution)/shard_map/ppermute | solution.py:65
  183.2 22.8 %collective-permute-start.13 = (bf16[128,4096]{0,1:T(8,128)(2,1)S(1)}, bf16[128,4096]{0,1:T(8,128)(2,1)S(1)}, u32[]{:S(2)}, u32[]{:S(2)}) collective-permute-start(bf16[128,4096]{0,1:T(8,128)(2,1)S(1)} %collective-permute-done.11), channel_id=1, source_target_pairs={{0,15},{1,0},{2,1},{3,2},{4,3},{5,4},{6,5},{7,6},{8,7},{9,8},{10,9... | collective-permute-start | bytes 3145736 | tf_op jit(solution)/shard_map/ppermute | solution.py:70
  201.8 22.2 %collective-permute-start.14 = (bf16[128,4096]{0,1:T(8,128)(2,1)S(1)}, bf16[128,4096]{0,1:T(8,128)(2,1)S(1)}, u32[]{:S(2)}, u32[]{:S(2)}) collective-permute-start(bf16[128,4096]{0,1:T(8,128)(2,1)S(1)} %collective-permute-done.12), channel_id=1, source_target_pairs={{0,1},{1,2},{2,3},{3,4},{4,5},{5,6},{6,7},{7,8},{8,9},{9,10},{10,1... | collective-permute-start | bytes 3145736 | tf_op jit(solution)/shard_map/ppermute | solution.py:65
  225.1 5.1 %copy-start.4 = (bf16[128,8,2,128]{3,2,1,0:T(2,128)(2,1)S(1)}, bf16[128,8,2,128]{3,2,1,0:T(2,128)(2,1)}, u32[]{:S(2)}) copy-start(bf16[128,8,2,128]{3,2,1,0:T(2,128)(2,1)} %reshape.141) | copy-start | bytes 1572868
  232.7 3.6 copy-start.2
  250.3 39.0 %copy-start.12 = (f32[2048]{0:T(1024)S(1)}, f32[2048]{0:T(1024)}, u32[]{:S(2)}) copy-start(f32[2048]{0:T(1024)} %param.22) | copy-start | bytes 24580
  255.9 91.7 %reduce-scatter.2.cloned.1.call-start = ((), (), s32[]{:S(2)}) async-start(), calls=%async_computation.4 | async-start | bytes 4718592 | tf_op jit(solution)/shard_map/reduce_scatter | solution.py:120
  297.3 52.6 %copy-start.8 = (f32[2048]{0:T(1024)S(1)}, f32[2048]{0:T(1024)}, u32[]{:S(2)}) copy-start(f32[2048]{0:T(1024)} %param.26) | copy-start | bytes 24580
  309.7 72.4 %all-gather.5.cloned.1.call-start = ((), (), s32[]{:S(2)}) async-start(), calls=%async_computation.5 | async-start | bytes 4718592 | tf_op jit(solution)/shard_map/all_gather | solution.py:129
  349.1 0.8 copy-start.5
  350.9 42.8 %copy-start.10 = (s32[1,256]{1,0:T(1,128)S(1)}, s32[1,256]{1,0:T(1,128)}, u32[]{:S(2)}) copy-start(s32[1,256]{1,0:T(1,128)} %param.28) | copy-start | bytes 3076
  350.9 43.6 %copy-start.11 = (s32[1,256]{1,0:T(1,128)S(1)}, s32[1,256]{1,0:T(1,128)}, u32[]{:S(2)}) copy-start(s32[1,256]{1,0:T(1,128)} %param.29) | copy-start | bytes 3076
  388.9 25.9 %all-to-all-start = ((bf16[8,128,768]{2,1,0:T(8,128)(2,1)}), bf16[8,128,768]{2,1,0:T(8,128)(2,1)}, u32[]{:S(2)}, u32[]{:S(2)}) async-start(bf16[8,128,768]{2,1,0:T(8,128)(2,1)} %bitcast.71), calls=%async_computation.1 | async-start | bytes 3145728 | tf_op jit(solution)/shard_map/all_to_all | solution.py:133
  416.3 1.2 copy-start.3
  421.4 24.4 %all-to-all-start.1 = ((bf16[16,1,8,4096]{3,2,1,0:T(8,128)(2,1)}), bf16[16,1,8,4096]{3,2,1,0:T(8,128)(2,1)}, u32[]{:S(2)}, u32[]{:S(2)}) async-start(bf16[16,1,8,4096]{3,2,1,0:T(8,128)(2,1)} %bitcast.69), calls=%async_computation.2 | async-start | bytes 2097152 | tf_op jit(solution)/shard_map/all_to_all | solution.py:144
Sparse Core Ops, SparseCore 0:
  256.1 30.0 all-gather.2
  309.8 37.7 reduce-scatter.1
  351.0 31.0 all-gather.4
